TPU v7x, 32 devices: a whole 2x2x4 slice. The times are simulated.
32 devices in a mesh: fsdp: 16 (over z, y, core), seq: 2 (over x).
Axes of the slice: x: 2, y: 2, z: 4, core: 2. Of those that a mesh axis runs over, the one named last changes fastest.
Arguments:
- tokens: bfloat16 [16, 1024, 1024], P('fsdp', 'seq'), may hold values from -6 to 6
- condition: bfloat16 [16, 1024], P('fsdp'), may hold values from -6 to 6
- w_ada: bfloat16 [1024, 6144], P('fsdp'), may hold values from -0.1875 to 0.1875
- b_ada: bfloat16 [6144], P('fsdp'), may hold values from -3 to 3
- w_qkv: bfloat16 [1024, 3072], P('fsdp'), may hold values from -0.1875 to 0.1875
- b_qv: bfloat16 [2048], P('fsdp'), may hold values from -1.1953125 to 1.1953125
- w_proj: bfloat16 [1024, 1024], P('fsdp'), may hold values from -0.1875 to 0.1875
- b_proj: bfloat16 [1024], P('fsdp'), may hold values from -1.1953125 to 1.1953125
- w_fc1: bfloat16 [1024, 4096], P('fsdp'), may hold values from -0.1875 to 0.1875
- b_fc1: bfloat16 [4096], P('fsdp'), may hold values from -1.1953125 to 1.1953125
- w_fc2: bfloat16 [4096, 1024], P('fsdp'), may hold values from -0.09375 to 0.09375
- b_fc2: bfloat16 [1024], P('fsdp'), may hold values from -1.1953125 to 1.1953125
- cotangent: bfloat16 [16, 1024, 1024], P('fsdp', 'seq'), may hold values from -6 to 6
Outputs:
- out_tokens: bfloat16 [16, 1024, 1024], P('fsdp', 'seq')
- grad_tokens: float32 [16, 1024, 1024], P('fsdp', 'seq')
- grad_condition: float32 [16, 1024], P('fsdp')
- grad_w_ada: float32 [1024, 6144], P('fsdp')
- grad_b_ada: float32 [6144], P('fsdp')
- grad_w_qkv: float32 [1024, 3072], P('fsdp')
- grad_b_qv: float32 [2048], P('fsdp')
- grad_w_proj: float32 [1024, 1024], P('fsdp')
- grad_b_proj: float32 [1024], P('fsdp')
- grad_w_fc1: float32 [1024, 4096], P('fsdp')
- grad_b_fc1: float32 [4096], P('fsdp')
- grad_w_fc2: float32 [4096, 1024], P('fsdp')
- grad_b_fc2: float32 [1024], P('fsdp')
All inputs are finite; a program needn't handle non-finite values.
Results may differ from a plain program's by a relative error of at most 0.018.
The roundings to bfloat16 on the way count: a program that leaves them out, or rounds other values in their place, can miss the bound.
Values may be sent and summed in bfloat16 or wider, within the bound.
A program may use at most 256 MiB of HBM per device.

v0:
```python
from functools import partial
import jax
import jax.numpy as jnp
from jax import lax
from jax.sharding import PartitionSpec as P

HD = 64
norm_eps = 1e-06
block_rows = 512


def layer_norm(values):
    center = values - jnp.mean(values, axis=-1, keepdims=True)
    rscale = lax.rsqrt(jnp.mean(center * center, axis=-1, keepdims=True) + norm_eps)
    return (center * rscale, rscale)


def norm_back(upstream, normed, rscale):
    mean_up = jnp.mean(upstream, axis=-1, keepdims=True)
    mean_cross = jnp.mean(upstream * normed, axis=-1, keepdims=True)
    return rscale * (upstream - mean_up - normed * mean_cross)


def attend_forward(queries, keys_all, values_all):
    seq_len = keys_all.shape[1]
    rows = min(block_rows, seq_len)
    score_scale = queries.shape[-1] ** (-0.5)
    outputs = []
    totals = []
    for offset in range(0, seq_len, rows):
        q_block = queries[:, offset : offset + rows]
        raw_scores = jnp.einsum(
            "bqhd,bkhd->bhqk", q_block, keys_all, preferred_element_type=jnp.float32
        )
        scores = raw_scores * score_scale
        row_max = jnp.max(scores, axis=-1, keepdims=True)
        shifted = jnp.exp(scores - row_max)
        row_total = jnp.sum(shifted, axis=-1, keepdims=True)
        attn_prob = (shifted / row_total).astype(jnp.bfloat16)
        block_out = jnp.einsum(
            "bhqk,bkhd->bqhd", attn_prob, values_all, preferred_element_type=jnp.float32
        )
        outputs.append(block_out.astype(jnp.bfloat16))
        totals.append(row_max + jnp.log(row_total))
    return (jnp.concatenate(outputs, axis=1), jnp.concatenate(totals, axis=2))


def attend_backward(queries, keys_all, values_all, log_total, d_out):
    seq_len = keys_all.shape[1]
    rows = min(block_rows, seq_len)
    score_scale = queries.shape[-1] ** (-0.5)
    grad_keys = jnp.zeros(keys_all.shape, jnp.float32)
    grad_values = jnp.zeros(values_all.shape, jnp.float32)
    grad_queries = []
    for offset in range(0, seq_len, rows):
        q_block = queries[:, offset : offset + rows]
        d_block = d_out[:, offset : offset + rows]
        raw_scores = jnp.einsum(
            "bqhd,bkhd->bhqk", q_block, keys_all, preferred_element_type=jnp.float32
        )
        attn_prob = jnp.exp(raw_scores * score_scale - log_total[:, :, offset : offset + rows])
        grad_values = grad_values + jnp.einsum(
            "bhqk,bqhd->bkhd",
            attn_prob.astype(jnp.bfloat16),
            d_block,
            preferred_element_type=jnp.float32,
        )
        d_prob = jnp.einsum(
            "bqhd,bkhd->bhqk", d_block, values_all, preferred_element_type=jnp.float32
        )
        center = jnp.sum(attn_prob * d_prob, axis=-1, keepdims=True)
        d_raw = (attn_prob * (d_prob - center) * score_scale).astype(jnp.bfloat16)
        grad_queries.append(
            jnp.einsum("bhqk,bkhd->bqhd", d_raw, keys_all, preferred_element_type=jnp.float32)
        )
        grad_keys = grad_keys + jnp.einsum(
            "bhqk,bqhd->bkhd", d_raw, q_block, preferred_element_type=jnp.float32
        )
    grad_q = jnp.concatenate(grad_queries, axis=1).astype(jnp.bfloat16)
    return (grad_q, grad_keys.astype(jnp.bfloat16), grad_values.astype(jnp.bfloat16))


def on_device(
    tokens,
    condition,
    w_ada,
    b_ada,
    w_qkv,
    b_qv,
    w_proj,
    b_proj,
    w_fc1,
    b_fc1,
    w_fc2,
    b_fc2,
    cotangent,
):
    latents, local_len, model_width = tokens.shape
    groups = lax.axis_size("seq")
    head_dim = HD
    group_width = model_width // groups
    per_group = group_width // head_dim
    ada_w, ada_b, qkv_w, qv_b, proj_w, proj_b, fc1_w, fc1_b, fc2_w, fc2_b = (
        lax.all_gather(w_ada, "fsdp", axis=0, tiled=True),
        lax.all_gather(b_ada, "fsdp", axis=0, tiled=True),
        lax.all_gather(w_qkv, "fsdp", axis=0, tiled=True),
        lax.all_gather(b_qv, "fsdp", axis=0, tiled=True),
        lax.all_gather(w_proj, "fsdp", axis=0, tiled=True),
        lax.all_gather(b_proj, "fsdp", axis=0, tiled=True),
        lax.all_gather(w_fc1, "fsdp", axis=0, tiled=True),
        lax.all_gather(b_fc1, "fsdp", axis=0, tiled=True),
        lax.all_gather(w_fc2, "fsdp", axis=0, tiled=True),
        lax.all_gather(b_fc2, "fsdp", axis=0, tiled=True),
    )
    tokens_f = tokens.astype(jnp.float32)
    lifted, silu_back = jax.vjp(jax.nn.silu, condition.astype(jnp.float32))
    lifted_b = lifted.astype(jnp.bfloat16)
    modulation = jnp.dot(lifted_b, ada_w, preferred_element_type=jnp.float32) + ada_b.astype(
        jnp.float32
    )
    shift_one, scale_one, gate_one, shift_two, scale_two, gate_two = jnp.split(
        modulation[:, None, :], 6, axis=-1
    )
    normed_one, rscale_one = layer_norm(tokens_f)
    hidden_one = (normed_one * (1.0 + scale_one) + shift_one).astype(jnp.bfloat16)
    qkv_bias = jnp.concatenate(
        [qv_b[:model_width], jnp.zeros((model_width,), jnp.bfloat16), qv_b[model_width:]]
    ).astype(jnp.float32)
    qkv_tok = (jnp.dot(hidden_one, qkv_w, preferred_element_type=jnp.float32) + qkv_bias).astype(
        jnp.bfloat16
    )
    spread = lax.all_to_all(
        qkv_tok.reshape(latents, local_len, 3, groups, group_width),
        "seq",
        split_axis=3,
        concat_axis=1,
        tiled=True,
    )
    seq_len = spread.shape[1]
    queries = spread[:, :, 0, 0].reshape(latents, seq_len, per_group, head_dim)
    keys_all = spread[:, :, 1, 0].reshape(latents, seq_len, per_group, head_dim)
    values_all = spread[:, :, 2, 0].reshape(latents, seq_len, per_group, head_dim)
    attn_out, log_total = attend_forward(queries, keys_all, values_all)
    returned = lax.all_to_all(
        attn_out.reshape(latents, seq_len, 1, group_width),
        "seq",
        split_axis=1,
        concat_axis=2,
        tiled=True,
    )
    attn_tok = returned.reshape(latents, local_len, model_width)
    branch = jnp.dot(attn_tok, proj_w, preferred_element_type=jnp.float32) + proj_b.astype(
        jnp.float32
    )
    middle = tokens_f + gate_one * branch
    normed_two, rscale_two = layer_norm(middle)
    hidden_two = (normed_two * (1.0 + scale_two) + shift_two).astype(jnp.bfloat16)
    pre_act = jnp.dot(hidden_two, fc1_w, preferred_element_type=jnp.float32) + fc1_b.astype(
        jnp.float32
    )
    act_f, gelu_back = jax.vjp(partial(jax.nn.gelu, approximate=True), pre_act)
    act_b = act_f.astype(jnp.bfloat16)
    mlp_out = jnp.dot(act_b, fc2_w, preferred_element_type=jnp.float32) + fc2_b.astype(jnp.float32)
    result = (middle + gate_two * mlp_out).astype(jnp.bfloat16)
    grad_out = cotangent.astype(jnp.float32)
    d_gate_two = jnp.sum(grad_out * mlp_out, axis=1)
    d_mlp = (grad_out * gate_two).astype(jnp.bfloat16)
    grad_fc2 = jnp.einsum("btf,btd->fd", act_b, d_mlp, preferred_element_type=jnp.float32)
    bias_fc2 = jnp.sum(d_mlp, axis=(0, 1), dtype=jnp.float32)
    d_act = jnp.einsum("btd,fd->btf", d_mlp, fc2_w, preferred_element_type=jnp.float32)
    d_pre = gelu_back(d_act)[0].astype(jnp.bfloat16)
    grad_fc1 = jnp.einsum("btd,btf->df", hidden_two, d_pre, preferred_element_type=jnp.float32)
    bias_fc1 = jnp.sum(d_pre, axis=(0, 1), dtype=jnp.float32)
    d_hidden_two = jnp.einsum("btf,df->btd", d_pre, fc1_w, preferred_element_type=jnp.float32)
    d_shift_two = jnp.sum(d_hidden_two, axis=1)
    d_scale_two = jnp.sum(d_hidden_two * normed_two, axis=1)
    d_middle = grad_out + norm_back(d_hidden_two * (1.0 + scale_two), normed_two, rscale_two)
    d_gate_one = jnp.sum(d_middle * branch, axis=1)
    d_branch = (d_middle * gate_one).astype(jnp.bfloat16)
    grad_proj = jnp.einsum("btk,btd->kd", attn_tok, d_branch, preferred_element_type=jnp.float32)
    bias_proj = jnp.sum(d_branch, axis=(0, 1), dtype=jnp.float32)
    d_attn = jnp.einsum("btd,kd->btk", d_branch, proj_w, preferred_element_type=jnp.float32).astype(
        jnp.bfloat16
    )
    d_heads = lax.all_to_all(
        d_attn.reshape(latents, local_len, groups, group_width),
        "seq",
        split_axis=2,
        concat_axis=1,
        tiled=True,
    )
    d_heads = d_heads.reshape(latents, seq_len, per_group, head_dim)
    grad_q, grad_k, grad_v = attend_backward(queries, keys_all, values_all, log_total, d_heads)
    d_spread = jnp.stack([grad_q, grad_k, grad_v], axis=2).reshape(
        latents, seq_len, 3, 1, group_width
    )
    d_qkv = lax.all_to_all(d_spread, "seq", split_axis=1, concat_axis=3, tiled=True).reshape(
        latents, local_len, 3 * model_width
    )
    grad_qkv = jnp.einsum("btd,bte->de", hidden_one, d_qkv, preferred_element_type=jnp.float32)
    column_sums = jnp.sum(d_qkv, axis=(0, 1), dtype=jnp.float32)
    bias_qv = jnp.concatenate([column_sums[:model_width], column_sums[2 * model_width :]])
    d_hidden_one = jnp.einsum("bte,de->btd", d_qkv, qkv_w, preferred_element_type=jnp.float32)
    d_shift_one = jnp.sum(d_hidden_one, axis=1)
    d_scale_one = jnp.sum(d_hidden_one * normed_one, axis=1)
    grad_input = d_middle + norm_back(d_hidden_one * (1.0 + scale_one), normed_one, rscale_one)
    d_partial = jnp.concatenate(
        [d_shift_one, d_scale_one, d_gate_one, d_shift_two, d_scale_two, d_gate_two], axis=-1
    )
    d_modulation = lax.psum(d_partial, "seq").astype(jnp.bfloat16)
    d_lifted = jnp.einsum("be,ce->bc", d_modulation, ada_w, preferred_element_type=jnp.float32)
    grad_condition = silu_back(d_lifted)[0]
    grad_ada = jnp.einsum("bc,be->ce", lifted_b, d_modulation, preferred_element_type=jnp.float32)
    bias_ada = jnp.sum(d_modulation, axis=0, dtype=jnp.float32)
    total_ada, total_bada = (
        lax.psum_scatter(
            grad_ada.astype(jnp.bfloat16), "fsdp", scatter_dimension=0, tiled=True
        ).astype(jnp.float32),
        lax.psum_scatter(
            bias_ada.astype(jnp.bfloat16), "fsdp", scatter_dimension=0, tiled=True
        ).astype(jnp.float32),
    )
    shard_qkv, shard_bqv, shard_proj, shard_bproj, shard_fc1, shard_bfc1, shard_fc2, shard_bfc2 = (
        lax.psum_scatter(grad_qkv, "fsdp", scatter_dimension=0, tiled=True),
        lax.psum_scatter(bias_qv, "fsdp", scatter_dimension=0, tiled=True),
        lax.psum_scatter(grad_proj, "fsdp", scatter_dimension=0, tiled=True),
        lax.psum_scatter(bias_proj, "fsdp", scatter_dimension=0, tiled=True),
        lax.psum_scatter(grad_fc1, "fsdp", scatter_dimension=0, tiled=True),
        lax.psum_scatter(bias_fc1, "fsdp", scatter_dimension=0, tiled=True),
        lax.psum_scatter(grad_fc2, "fsdp", scatter_dimension=0, tiled=True),
        lax.psum_scatter(bias_fc2, "fsdp", scatter_dimension=0, tiled=True),
    )
    total_qkv, total_bqv, total_proj, total_bproj, total_fc1, total_bfc1, total_fc2, total_bfc2 = (
        lax.psum(
            (
                shard_qkv,
                shard_bqv,
                shard_proj,
                shard_bproj,
                shard_fc1,
                shard_bfc1,
                shard_fc2,
                shard_bfc2,
            ),
            "seq",
        )
    )
    return (
        result,
        grad_input,
        grad_condition,
        total_ada,
        total_bada,
        total_qkv,
        total_bqv,
        total_proj,
        total_bproj,
        total_fc1,
        total_bfc1,
        total_fc2,
        total_bfc2,
    )


def solution(mesh):
    return jax.shard_map(
        on_device,
        mesh=mesh,
        in_specs=(
            P("fsdp", "seq", None),
            P("fsdp", None),
            P("fsdp", None),
            P("fsdp"),
            P("fsdp", None),
            P("fsdp"),
            P("fsdp", None),
            P("fsdp"),
            P("fsdp", None),
            P("fsdp"),
            P("fsdp", None),
            P("fsdp"),
            P("fsdp", "seq", None),
        ),
        out_specs=(
            P("fsdp", "seq", None),
            P("fsdp", "seq", None),
            P("fsdp", None),
            P("fsdp", None),
            P("fsdp"),
            P("fsdp", None),
            P("fsdp"),
            P("fsdp", None),
            P("fsdp"),
            P("fsdp", None),
            P("fsdp"),
            P("fsdp", None),
            P("fsdp"),
        ),
        check_vma=False,
    )
```

profile of v0, /device:TPU:0, one launch (start us, length us, event | category | flops | bytes accessed | tf_op | source)
XLA Modules:
  0.0 1429.1 jit_solution(12914743900525769951)
XLA Ops:
  12.0 23.8 %all-gather.1 = bf16[16,1,128]{2,1,0:T(2,128)(2,1)S(1)} all-gather(bf16[1,1,128]{2,1,0:T(2,128)(2,1)} %bitcast.251), channel_id=1, replica_groups=mesh['fsdp'=16,'seq'=2] {'fsdp'}, dimensions={0}, use_global_device_ids=true | all-gather | bytes 4352 | tf_op jit(solution)/shard_map/all_gather | solution.py:107
  36.5 18.1 %all-gather = bf16[16,1,384]{2,1,0:T(2,128)(2,1)S(1)} all-gather(bf16[1,1,384]{2,1,0:T(2,128)(2,1)S(1)} %reshape.506), channel_id=1, replica_groups=mesh['fsdp'=16,'seq'=2] {'fsdp'}, dimensions={0}, use_global_device_ids=true | all-gather | bytes 13056 | tf_op jit(solution)/shard_map/all_gather | solution.py:105
  56.7 56.9 %all-gather.9.cloned.1.call-done = bf16[1024,6144]{1,0:T(8,128)(2,1)} async-done(((bf16[64,6144]{1,0:T(8,128)(2,1)}), bf16[1024,6144]{1,0:T(8,128)(2,1)}) %all-gather.9.cloned.1.call-update) | async-done | bytes 12582928 | tf_op jit(solution)/shard_map/all_gather | solution.py:104
  120.0 55.6 %all-gather.11.cloned.1.call-done = bf16[1024,3072]{1,0:T(8,128)(2,1)} async-done(((bf16[64,3072]{1,0:T(8,128)(2,1)}), bf16[1024,3072]{1,0:T(8,128)(2,1)}) %all-gather.11.cloned.1.call-update) | async-done | bytes 6291472 | tf_op jit(solution)/shard_map/all_gather | solution.py:106
  191.0 39.7 %all_to_all.63 = bf16[1,512,3,2,512]{4,1,2,0,3:T(8,128)(2,1)S(1)} all-to-all(bf16[1,512,3,2,512]{4,1,2,0,3:T(8,128)(2,1)S(1)} %copy.46), channel_id=1, replica_groups=mesh['fsdp'=16,'seq'=2] {'seq'}, dimensions={3} | all-to-all | bytes 6291456 | tf_op jit(solution)/shard_map/all_to_all | solution.py:132
  237.3 8.6 multiply_reduce_fusion.3
  275.9 9.0 reduce.38
  293.8 30.7 %all-reduce.10 = (bf16[1024]{0:T(1024)(128)(2,1)S(1)}, bf16[1024]{0:T(1024)(128)(2,1)S(1)}) all-reduce(bf16[1024]{0:T(1024)(128)(2,1)S(1)} %dynamic-update-slice, bf16[1024]{0:T(1024)(128)(2,1)S(1)} %dynamic-update-slice.1), channel_id=1, replica_groups=mesh['fsdp'=16,'seq'=2] {'fsdp'}, use_global_device_ids=true, to_apply=%add | all-reduce | flops 2048 | bytes 8192
  324.5 17.6 %all-gather.2 = bf16[16,1,256]{2,1,0:T(2,128)(2,1)S(1)} all-gather(bf16[1,1,256]{2,1,0:T(2,128)(2,1)S(1)} %reshape.510), channel_id=1, replica_groups=mesh['fsdp'=16,'seq'=2] {'fsdp'}, dimensions={0}, use_global_device_ids=true | all-gather | bytes 8704 | tf_op jit(solution)/shard_map/all_gather | solution.py:111
  356.6 12.0 fusion.122
  368.6 13.9 convert_reduce_fusion
  382.5 9.8 fusion.55
  393.1 10.4 convert_reduce_fusion.3
  418.4 9.5 all-to-all-done.2
  440.4 8.7 add_convert_fusion.1
  463.1 37.1 %fusion.64 = bf16[8,64,512]{2,1,0:T(8,128)(2,1)} fusion(bf16[1024,8,64]{0,2,1:T(8,128)(2,1)S(1)} %bitcast.199, f32[8,512,1024]{2,1,0:T(8,128)} %fusion.90, f32[8,512]{1,0:T(8,128)S(1)} %log_add_fusion, f32[8,512,1024]{2,1,0:T(8,128)} %copy-done), kind=kOutput, calls=%fused_computation.90 | convolution fusion | flops 574886912 | bytes 35143680 | tf_op jit(solution)/shard_map/bhqk,bkhd->bqhd/dot_general | solution.py:74
  511.8 36.6 %fusion.67 = bf16[8,64,512]{2,1,0:T(8,128)(2,1)S(1)} fusion(bf16[1024,8,64]{0,2,1:T(8,128)(2,1)S(1)} %bitcast.200, f32[8,512,1024]{2,1,0:T(8,128)} %fusion.89, f32[8,512]{1,0:T(8,128)S(1)} %log_add_fusion.1, f32[8,512,1024]{2,1,0:T(8,128)} %get-tuple-element.67), kind=kOutput, calls=%fused_computation.91 | convolution fusion | flops 574886912 | bytes 35143680 | tf_op jit(solution)/shard_map/bhqk,bkhd->bqhd/dot_general | solution.py:74
  550.4 30.7 %fusion.11 = f32[8,64,1024]{2,1,0:T(8,128)} fusion(f32[8,512,1024]{2,1,0:T(8,128)} %fusion.89, f32[8,512,1024]{2,1,0:T(8,128)} %get-tuple-element.67, f32[8,512]{1,0:T(8,128)S(1)} %log_add_fusion.1, bf16[1,1024,8,64]{1,3,2,0:T(8,128)(2,1)S(1)} %bitcast.210), kind=kOutput, calls=%fused_computation.21 | convolution fusion | flops 574624768 | bytes 69763072 | tf_op jit(solution)/shard_map/bhqk,bqhd->bkhd/dot_general | solution.py:76
  581.1 31.5 %add_convert_fusion.2 = bf16[8,64,1024]{2,1,0:T(8,128)(2,1)} fusion(f32[8,64,1024]{2,1,0:T(8,128)} %fusion.11, f32[8,512,1024]{2,1,0:T(8,128)} %fusion.90, f32[8,512]{1,0:T(8,128)S(1)} %log_add_fusion, f32[8,512,1024]{2,1,0:T(8,128)} %copy-done, bf16[1,1024,8,64]{1,3,2,0:T(8,128)(2,1)} %bitcast.208), kind=kOutput, calls=%fused_computation.82 | convolution fusion | flops 575673344 | bytes 70811648 | tf_op jit(solution)/shard_map/bhqk,bqhd->bkhd/dot_general | solution.py:76
  627.1 50.3 %all_to_all.64 = bf16[1,1024,3,1,512]{4,2,3,0,1:T(4,128)(2,1)S(1)} all-to-all(bf16[1,1024,3,1,512]{4,2,3,0,1:T(4,128)(2,1)S(1)} %pad_maximum_fusion), channel_id=1, replica_groups=mesh['fsdp'=16,'seq'=2] {'seq'}, dimensions={1} | all-to-all | bytes 6291456 | tf_op jit(solution)/shard_map/all_to_all | solution.py:197
  681.1 10.5 fusion.117
  691.7 18.5 %fusion.79 = f32[4096,1024]{1,0:T(8,128)} fusion(bf16[1,512,1024]{2,1,0:T(8,128)(2,1)} %param.25, f32[1024]{0:T(1024)S(1)} %bitcast.243, f32[512,4096]{1,0:T(8,128)} %fusion.122, f32[4096]{0:T(1024)S(1)} %bitcast.236), kind=kOutput, calls=%fused_computation.102 | convolution fusion | flops 4317511680 | bytes 26234880 | tf_op jit(solution)/shard_map/btf,btd->fd/dot_general | solution.py:168
  710.8 15.0 %fusion.120 = f32[1024,4096]{1,0:T(8,128)} fusion(bf16[512,4096]{1,0:T(8,128)(2,1)} %copy-done.37, f32[1,512,1024]{2,1,0:T(8,128)} %copy-done.9, f32[1024]{0:T(1024)S(1)} %bitcast.240, f32[1024]{0:T(1024)S(1)} %bitcast.230, f32[512]{0:T(512)S(1)} %add_rsqrt_fusion, f32[512]{0:T(512)S(1)} %broadcast_multiply_fusion.4), kind=kOutput, calls=%fused_computation.165 | convolution fusion | flops 4297588736 | bytes 23080960 | tf_op jit(solution)/shard_map/btd,btf->df/dot_general | solution.py:172
  728.3 61.3 %all-reduce.7 = (f32[2048]{0:T(1024)S(1)}, f32[1024]{0:T(1024)S(1)}, f32[4096]{0:T(1024)S(1)}, f32[1024]{0:T(1024)S(1)}) all-reduce(f32[2048]{0:T(1024)S(1)} %pad_maximum_fusion.2, f32[1024]{0:T(1024)S(1)} %get-tuple-element.47, f32[4096]{0:T(1024)S(1)} %copy-done.21, ...), channel_id=5, replica_groups=mesh['fsdp'=16,'seq'=2] {'fsdp'}, use_global_device_ids=true, to_apply=%region_26.27.clone | all-reduce | flops 8192 | bytes 65536
  800.8 9.9 all-reduce.8
  818.3 8.7 reduce-scatter.8.cloned.1.call-done
  827.0 180.7 %reduce-scatter.14.cloned.1.call-done = f32[256,1024]{1,0:T(8,128)} async-done(((f32[4096,1024]{1,0:T(8,128)}), f32[256,1024]{1,0:T(8,128)}) %reduce-scatter.14.cloned.1.call-update) | async-done | bytes 1048592 | tf_op jit(solution)/shard_map/reduce_scatter | solution.py:230
  1007.7 180.6 %reduce-scatter.12.cloned.1.call-done = f32[64,4096]{1,0:T(8,128)} async-done(((f32[1024,4096]{1,0:T(8,128)}), f32[64,4096]{1,0:T(8,128)}) %reduce-scatter.12.cloned.1.call-update) | async-done | bytes 1048592 | tf_op jit(solution)/shard_map/reduce_scatter | solution.py:228
  1188.9 61.3 %all-reduce.2 = bf16[6144]{0:T(1024)(128)(2,1)S(1)} all-reduce(bf16[6144]{0:T(1024)(128)(2,1)S(1)} %convert_reduce_fusion.5), channel_id=3, replica_groups=mesh['fsdp'=16,'seq'=2] {'fsdp'}, use_global_device_ids=true, to_apply=%region_22.23.clone | all-reduce | flops 6144 | bytes 24576
  1250.8 8.7 fusion.95
  1259.5 67.0 %reduce-scatter.6.cloned.1.call-done = bf16[64,6144]{1,0:T(8,128)(2,1)} async-done(((bf16[1024,6144]{1,0:T(8,128)(2,1)}), bf16[64,6144]{1,0:T(8,128)(2,1)}) %reduce-scatter.6.cloned.1.call-update) | async-done | bytes 786448 | tf_op jit(solution)/shard_map/reduce_scatter | solution.py:216
  1328.8 85.2 %all-reduce.13.cloned.1.call-done = (f32[64,3072]{1,0:T(8,128)}, f32[64,1024]{1,0:T(8,128)}, f32[64,4096]{1,0:T(8,128)}, f32[256,1024]{1,0:T(8,128)}) async-done(((f32[64,3072]{1,0:T(8,128)}, f32[64,1024]{1,0:T(8,128)}, f32[64,4096]{1,0:T(8,128)}, f32[256,1024]{1,0:T(8,128)}), (f32[64,3072]{1,0:T(8,128)}, f32[64,1024]{1,0:T(8,128)}, f32[64,4096]{1,0:T(8,128)}, ...) | async-done | bytes 3145744 | tf_op jit(solution)/shard_map/psum | solution.py:234
  (203 shorter events, 193.6 us)
Async XLA Ops:
  7.2 106.4 %all-gather.9.cloned.1.call-start = ((), (), s32[]{:S(2)}) async-start(), calls=%async_computation.9 | async-start | bytes 13369344 | tf_op jit(solution)/shard_map/all_gather | solution.py:104
  7.9 167.6 %all-gather.11.cloned.1.call-start = ((), (), s32[]{:S(2)}) async-start(), calls=%async_computation.10 | async-start | bytes 6684672 | tf_op jit(solution)/shard_map/all_gather | solution.py:106
  8.7 341.7 %all-gather.13.cloned.1.call-start = ((), (), s32[]{:S(2)}) async-start(), calls=%async_computation.11 | async-start | bytes 2228224 | tf_op jit(solution)/shard_map/all_gather | solution.py:108
  9.4 347.2 %all-gather.15.cloned.1.call-start = ((), (), s32[]{:S(2)}) async-start(), calls=%async_computation.12 | async-start | bytes 8912896 | tf_op jit(solution)/shard_map/all_gather | solution.py:110
  10.0 358.7 %all-gather.17.cloned.1.call-start = ((), (), s32[]{:S(2)}) async-start(), calls=%async_computation.13 | async-start | bytes 8912896 | tf_op jit(solution)/shard_map/all_gather | solution.py:112
  54.7 120.8 %copy-start.16 = (f32[512]{0:T(512)}, f32[512]{0:T(512)S(1)}, u32[]{:S(2)}) copy-start(f32[512]{0:T(512)S(1)} %broadcast_multiply_fusion.5) | copy-start | bytes 6148
  56.7 118.9 %copy-start.22 = (f32[512]{0:T(512)}, f32[512]{0:T(512)S(1)}, u32[]{:S(2)}) copy-start(f32[512]{0:T(512)S(1)} %add_rsqrt_fusion.1) | copy-start | bytes 6148
  56.7 118.9 %copy-start.2 = (bf16[1,512,1024]{2,1,0:T(8,128)(2,1)S(1)}, bf16[1,512,1024]{2,1,0:T(8,128)(2,1)}, u32[]{:S(2)}) copy-start(bf16[1,512,1024]{2,1,0:T(8,128)(2,1)} %param.13) | copy-start | bytes 3145732
  119.9 55.6 %copy-start.14 = (f32[1,1,1024]{2,1,0:T(1,128)}, f32[1,1,1024]{2,1,0:T(1,128)S(1)}, u32[]{:S(2)}) copy-start(f32[1,1,1024]{2,1,0:T(1,128)S(1)} %get-tuple-element.56) | copy-start | bytes 12292
  120.0 55.6 %copy-start.26 = (f32[1,1,1024]{2,1,0:T(1,128)}, f32[1,1,1024]{2,1,0:T(1,128)S(1)}, u32[]{:S(2)}) copy-start(f32[1,1,1024]{2,1,0:T(1,128)S(1)} %get-tuple-element.55) | copy-start | bytes 12292
  120.0 236.6 %copy-start.24 = (f32[1,1,1024]{2,1,0:T(1,128)}, f32[1,1,1024]{2,1,0:T(1,128)S(1)}, u32[]{:S(2)}) copy-start(f32[1,1,1024]{2,1,0:T(1,128)S(1)} %get-tuple-element.53) | copy-start | bytes 12292
  237.3 21.3 %copy-start = (f32[8,512,1024]{2,1,0:T(8,128)}, f32[8,512,1024]{2,1,0:T(8,128)S(1)}, u32[]{:S(2)}) copy-start(f32[8,512,1024]{2,1,0:T(8,128)S(1)} %get-tuple-element.65) | copy-start | bytes 50331652
  270.8 21.2 %copy-start.33 = (bf16[256]{0:T(256)(128)(2,1)S(1)}, bf16[256]{0:T(256)(128)(2,1)}, u32[]{:S(2)}) copy-start(bf16[256]{0:T(256)(128)(2,1)} %param.22) | copy-start | bytes 1540
  270.8 21.3 %copy-start.29 = (u32[32]{0:T(128)S(1)}, u32[32]{0:T(128)}, u32[]{:S(2)}) copy-start(u32[32]{0:T(128)} %constant.40) | copy-start | bytes 388
  270.8 22.5 %copy-start.34 = (bf16[64]{0:T(256)(128)(2,1)S(1)}, bf16[64]{0:T(256)(128)(2,1)}, u32[]{:S(2)}) copy-start(bf16[64]{0:T(256)(128)(2,1)} %param.24) | copy-start | bytes 388
  270.8 22.8 %copy-start.35 = (bf16[64]{0:T(256)(128)(2,1)S(1)}, bf16[64]{0:T(256)(128)(2,1)}, u32[]{:S(2)}) copy-start(bf16[64]{0:T(256)(128)(2,1)} %param.20) | copy-start | bytes 388
  275.3 75.0 %copy-start.3 = (bf16[1,512,1024]{2,1,0:T(8,128)(2,1)S(1)}, bf16[1,512,1024]{2,1,0:T(8,128)(2,1)}, u32[]{:S(2)}) copy-start(bf16[1,512,1024]{2,1,0:T(8,128)(2,1)} %param.13) | copy-start | bytes 3145732
  287.5 54.6 %all-to-all-start.1 = ((bf16[2,2,131072]{2,1,0:T(2,128)(2,1)}), bf16[2,2,131072]{2,1,0:T(2,128)(2,1)}, u32[]{:S(2)}, u32[]{:S(2)}) async-start(bf16[2,2,131072]{2,1,0:T(2,128)(2,1)} %reshape.533), calls=%async_computation.1 | async-start | bytes 2097152 | tf_op jit(solution)/shard_map/all_to_all | solution.py:144
  324.5 30.5 %copy-start.18 = (f32[1024]{0:T(1024)}, f32[1024]{0:T(1024)S(1)}, u32[]{:S(2)}) copy-start(f32[1024]{0:T(1024)S(1)} %convert_element_type.179) | copy-start | bytes 12292
  356.6 12.0 copy-start.32
  368.6 13.9 copy-start.10
  393.1 11.4 copy-start.31
  409.8 18.1 %all-to-all-start.2 = ((bf16[1,512,2,512]{3,1,0,2:T(8,128)(2,1)}), bf16[1,512,2,512]{3,1,0,2:T(8,128)(2,1)S(1)}, u32[]{:S(2)}, u32[]{:S(2)}) async-start(bf16[1,512,2,512]{3,1,0,2:T(8,128)(2,1)} %copy.53), calls=%async_computation.2 | async-start | bytes 2097152 | tf_op jit(solution)/shard_map/all_to_all | solution.py:185
  413.3 404.9 %reduce-scatter.10.cloned.1.call-start = ((), (), s32[]{:S(2)}) async-start(), calls=%async_computation.16 | async-start | bytes 4456448 | tf_op jit(solution)/shard_map/reduce_scatter | solution.py:226
  418.4 408.6 %reduce-scatter.8.cloned.1.call-start = ((), (), s32[]{:S(2)}) async-start(), calls=%async_computation.15 | async-start | bytes 13369344 | tf_op jit(solution)/shard_map/reduce_scatter | solution.py:224
  511.8 38.6 %copy-start.8 = (bf16[1,1024,1,1,512]{1,4,3,2,0:T(8,128)(2,1)S(1)}, bf16[1,1024,1,1,512]{1,4,3,2,0:T(8,128)(2,1)}, u32[]{:S(2)}) copy-start(bf16[1,1024,1,1,512]{1,4,3,2,0:T(8,128)(2,1)} %copy.49) | copy-start | bytes 3145732
  581.1 37.5 %copy-start.5 = (bf16[1,1024,1,1,512]{4,2,3,0,1:T(2,128)(2,1)S(1)}, bf16[1,1024,1,1,512]{4,2,3,0,1:T(2,128)(2,1)}, u32[]{:S(2)}) copy-start(bf16[1,1024,1,1,512]{4,2,3,0,1:T(2,128)(2,1)} %copy.58) | copy-start | bytes 3145732
  581.1 37.5 %copy-start.6 = (bf16[1,512,1,1,512]{4,2,3,0,1:T(2,128)(2,1)S(1)}, bf16[1,512,1,1,512]{4,2,3,0,1:T(2,128)(2,1)}, u32[]{:S(2)}) copy-start(bf16[1,512,1,1,512]{4,2,3,0,1:T(2,128)(2,1)} %copy.56) | copy-start | bytes 1572868
  691.6 316.1 %reduce-scatter.14.cloned.1.call-start = ((), (), s32[]{:S(2)}) async-start(), calls=%async_computation.18 | async-start | bytes 17825792 | tf_op jit(solution)/shard_map/reduce_scatter | solution.py:230
  710.2 478.1 %reduce-scatter.12.cloned.1.call-start = ((), (), s32[]{:S(2)}) async-start(), calls=%async_computation.17 | async-start | bytes 17825792 | tf_op jit(solution)/shard_map/reduce_scatter | solution.py:228
  725.9 600.6 %reduce-scatter.6.cloned.1.call-start = ((), (), s32[]{:S(2)}) async-start(), calls=%async_computation.14 | async-start | bytes 13369344 | tf_op jit(solution)/shard_map/reduce_scatter | solution.py:216
  818.2 595.9 %all-reduce.13.cloned.1.call-start = ((), (), s32[]{:S(2)}) async-start(), calls=%async_computation.19 | async-start | bytes 6291456 | tf_op jit(solution)/shard_map/psum | solution.py:234
  (19 other events, 94.2 us)
Sparse Core Ops, SparseCore 0:
  10.3 103.2 all-gather.8
  115.9 59.6 all-gather.10
  177.7 40.1 all-gather.12
  219.9 73.0 all-gather.14
  295.0 73.1 all-gather.16
  418.5 72.8 reduce-scatter.9
  691.7 135.2 reduce-scatter.7
  831.1 176.5 reduce-scatter.13
  1011.9 176.4 reduce-scatter.11
  1192.2 134.2 reduce-scatter.5
  1328.9 85.0 all-reduce.12
where the time goes:
time: 1440 us; the launch traced here: 1430 us
  waiting for transfers between devices  647 us (45%)
  matrix products  326 us (23%)
  blocking collectives  313 us (22%)
  local copies, waits for them, and re-layouts  73.4 us (5%)
  other arithmetic  42.9 us (3%)
  between operations  17.8 us (1%)
    reduce_scatter x1, waiting for transfers between devices, on_device(): lax.psum_scatter(grad_fc2, 'fsdp', scatter_dimension=0, tiled=True)  181 us
    reduce_scatter x1, waiting for transfers between devices, on_device(): lax.psum_scatter(grad_fc1, 'fsdp', scatter_dimension=0, tiled=True)  181 us
    unnamed x3, blocking collectives  153 us
    psum x1, waiting for transfers between devices, on_device(): lax.psum((shard_qkv, shard_bqv, shard_proj, shard_bproj, shard_fc1, shard...  85.2 us
    dot_general x2, matrix products, attend_backward(): jnp.einsum('bhqk,bkhd->bqhd', d_raw, keys_all, preferred_element_type=jnp...  73.6 us
    reduce_scatter x1, waiting for transfers between devices, on_device(): lax.psum_scatter(grad_ada.astype(jnp.bfloat16), 'fsdp', scatter_dimension...  67 us
    dot_general x2, matrix products, attend_backward(): jnp.einsum('bhqk,bqhd->bkhd', d_raw, q_block, preferred_element_type=jnp....  62.2 us
    all_gather x1, waiting for transfers between devices, on_device(): lax.all_gather(w_ada, 'fsdp', axis=0, tiled=True)  56.9 us
  transfers between devices with their start and end apart: 13, of which 8 were waited for; matrix products, arithmetic and copies ran while one was open for 27% of the time, Pallas kernels for 0%

commit v1 on v0

--- a/solution.py
+++ b/solution.py
@@ -100,8 +100,33 @@
     head_dim = HD
     group_width = model_width // groups
     per_group = group_width // head_dim
+
+    def render_strips_all_on_mesh(t0, mesh_dim):
+        val2, far_arr, value_now = (lax.axis_size(mesh_dim), lax.axis_index(mesh_dim), t0.shape[0])
+        items = []
+        for idx in range(val2):
+            items.append((idx, (idx + 1) % val2))
+        crops = []
+        for idx in range(val2):
+            crops.append((idx, (idx - 1) % val2))
+        w2 = jnp.zeros((*t0.shape[:0], val2 * value_now, *t0.shape[1:]), t0.dtype)
+        w2 = lax.dynamic_update_slice_in_dim(w2, t0, far_arr * value_now, axis=0)
+        step_out = field_out = t0
+        kept_arr = val2 // 2
+        for c in range(1, kept_arr + 1):
+            step_out = lax.ppermute(step_out, axis_name=mesh_dim, perm=items)
+            w2 = lax.dynamic_update_slice_in_dim(
+                w2, step_out, (far_arr - c) % val2 * value_now, axis=0
+            )
+            if c < val2 - kept_arr:
+                field_out = lax.ppermute(field_out, axis_name=mesh_dim, perm=crops)
+                w2 = lax.dynamic_update_slice_in_dim(
+                    w2, field_out, (far_arr + c) % val2 * value_now, axis=0
+                )
+        return w2
+
     ada_w, ada_b, qkv_w, qv_b, proj_w, proj_b, fc1_w, fc1_b, fc2_w, fc2_b = (
-        lax.all_gather(w_ada, "fsdp", axis=0, tiled=True),
+        render_strips_all_on_mesh(w_ada, "fsdp"),
         lax.all_gather(b_ada, "fsdp", axis=0, tiled=True),
         lax.all_gather(w_qkv, "fsdp", axis=0, tiled=True),
         lax.all_gather(b_qv, "fsdp", axis=0, tiled=True),

time: 1440 us -> 1500 us (1.042)
  starting transfers between devices: 8.89 us -> 115 us
  waiting for transfers between devices: 647 us -> 574 us
  local copies, waits for them, and re-layouts: 73.4 us -> 94.4 us
    ppermute x0 -> x15, starting transfers between devices: none -> 107 us  [the longest x8 89.3 us: render_strips_all_on_mesh(): step_out = lax.ppermute(step_out, axis_name=mesh_dim, perm=items)]
    all_gather x1 -> x0, waiting for transfers between devices: 56.9 us -> none  [on_device(): lax.all_gather(w_ada, 'fsdp', axis=0, tiled=True)]
    all_gather x1, waiting for transfers between devices: 55.6 us -> 0.02 us  [on_device(): lax.all_gather(w_qkv, 'fsdp', axis=0, tiled=True)]
    ppermute x0 -> x15, waiting for transfers between devices: none -> 40.4 us  [the longest x8 26.1 us: render_strips_all_on_mesh(): step_out = lax.ppermute(step_out, axis_name=mesh_dim, perm=items)]
    dynamic_update_slice x0 -> x16, local copies, waits for them, and re-layouts: none -> 15.3 us  [the longest x8 7.69 us: render_strips_all_on_mesh(): lax.dynamic_update_slice_in_dim(w2, step_out, (far_arr - c) % val2 * valu...]
  transfers between devices with their start and end apart: 13 -> 27, of which waited for: 8 -> 12; matrix products, arithmetic and copies ran while one was open for 27% -> 27% of each run, Pallas kernels for 0% -> 0%
where the time goes in v1:
time: 1500 us; the launch traced here: 1490 us
  waiting for transfers between devices  574 us (38%)
  matrix products  325 us (22%)
  blocking collectives  318 us (21%)
  starting transfers between devices  115 us (8%)
  local copies, waits for them, and re-layouts  94.4 us (6%)
  other arithmetic  42.6 us (3%)
  between operations  18.5 us (1%)
    reduce_scatter x1, waiting for transfers between devices, on_device(): lax.psum_scatter(grad_fc2, 'fsdp', scatter_dimension=0, tiled=True)  181 us
    reduce_scatter x1, waiting for transfers between devices, on_device(): lax.psum_scatter(grad_fc1, 'fsdp', scatter_dimension=0, tiled=True)  181 us
    unnamed x3, blocking collectives  153 us
    ppermute x8, starting transfers between devices, render_strips_all_on_mesh(): step_out = lax.ppermute(step_out, axis_name=mesh_dim, perm=items)  89.3 us
    psum x1, waiting for transfers between devices, on_device(): lax.psum((shard_qkv, shard_bqv, shard_proj, shard_bproj, shard_fc1, shard...  85.1 us
    dot_general x2, matrix products, attend_backward(): jnp.einsum('bhqk,bkhd->bqhd', d_raw, keys_all, preferred_element_type=jnp...  73.7 us
    reduce_scatter x1, waiting for transfers between devices, on_device(): lax.psum_scatter(grad_ada.astype(jnp.bfloat16), 'fsdp', scatter_dimension...  67.1 us
    dot_general x2, matrix products, attend_backward(): jnp.einsum('bhqk,bqhd->bkhd', d_raw, q_block, preferred_element_type=jnp....  62.2 us
  transfers between devices with their start and end apart: 27, of which 12 were waited for; matrix products, arithmetic and copies ran while one was open for 27% of the time, Pallas kernels for 0%

profile of v1, /device:TPU:0, one launch (start us, length us, event | category | flops | bytes accessed | tf_op | source)
XLA Modules:
  0.0 1487.1 jit_solution(2591025881636995042)
XLA Ops:
  19.1 28.6 %all-gather.1 = bf16[16,1,128]{2,1,0:T(2,128)(2,1)S(1)} all-gather(bf16[1,1,128]{2,1,0:T(2,128)(2,1)} %bitcast.251), channel_id=1, replica_groups=mesh['fsdp'=16,'seq'=2] {'fsdp'}, dimensions={0}, use_global_device_ids=true | all-gather | bytes 4352 | tf_op jit(solution)/shard_map/all_gather | solution.py:132
  47.7 19.1 %all-gather = bf16[16,1,384]{2,1,0:T(2,128)(2,1)S(1)} all-gather(bf16[1,1,384]{2,1,0:T(2,128)(2,1)S(1)} %reshape.506), channel_id=1, replica_groups=mesh['fsdp'=16,'seq'=2] {'fsdp'}, dimensions={0}, use_global_device_ids=true | all-gather | bytes 13056 | tf_op jit(solution)/shard_map/all_gather | solution.py:130
  89.0 14.3 collective-permute-start.4
  107.1 20.2 %collective-permute-start.6 = (bf16[64,6144]{1,0:T(8,128)(2,1)S(1)}, bf16[64,6144]{1,0:T(8,128)(2,1)S(1)}, u32[]{:S(2)}, u32[]{:S(2)}) collective-permute-start(bf16[64,6144]{1,0:T(8,128)(2,1)S(1)} %collective-permute-done.4), channel_id=1, source_target_pairs={{0,2},{2,4},{4,6},{6,8},{8,10},{10,12},{12,14},{14,16},{16,18},{18... | collective-permute-start | bytes 2359304 | tf_op jit(solution)/shard_map/ppermute | solution.py:117
  129.2 17.6 %collective-permute-start.8 = (bf16[64,6144]{1,0:T(8,128)(2,1)S(1)}, bf16[64,6144]{1,0:T(8,128)(2,1)S(1)}, u32[]{:S(2)}, u32[]{:S(2)}) collective-permute-start(bf16[64,6144]{1,0:T(8,128)(2,1)S(1)} %collective-permute-done.6), channel_id=1, source_target_pairs={{0,2},{2,4},{4,6},{6,8},{8,10},{10,12},{12,14},{14,16},{16,18},{18... | collective-permute-start | bytes 2359304 | tf_op jit(solution)/shard_map/ppermute | solution.py:117
  148.7 15.1 %collective-permute-start.10 = (bf16[64,6144]{1,0:T(8,128)(2,1)S(1)}, bf16[64,6144]{1,0:T(8,128)(2,1)S(1)}, u32[]{:S(2)}, u32[]{:S(2)}) collective-permute-start(bf16[64,6144]{1,0:T(8,128)(2,1)S(1)} %collective-permute-done.8), channel_id=1, source_target_pairs={{0,2},{2,4},{4,6},{6,8},{8,10},{10,12},{12,14},{14,16},{16,18},{18... | collective-permute-start | bytes 2359304 | tf_op jit(solution)/shard_map/ppermute | solution.py:117
  178.6 11.9 collective-permute-start.12
  192.4 17.0 %collective-permute-done.12 = bf16[64,6144]{1,0:T(8,128)(2,1)S(1)} collective-permute-done((bf16[64,6144]{1,0:T(8,128)(2,1)S(1)}, bf16[64,6144]{1,0:T(8,128)(2,1)S(1)}, u32[]{:S(2)}, u32[]{:S(2)}) %collective-permute-start.12) | collective-permute-done | bytes 786464 | tf_op jit(solution)/shard_map/ppermute | solution.py:117
  209.4 10.3 collective-permute-start.14
  252.7 39.6 %all_to_all.63 = bf16[1,512,3,2,512]{4,1,2,0,3:T(8,128)(2,1)S(1)} all-to-all(bf16[1,512,3,2,512]{4,1,2,0,3:T(8,128)(2,1)S(1)} %copy.46), channel_id=1, replica_groups=mesh['fsdp'=16,'seq'=2] {'seq'}, dimensions={3} | all-to-all | bytes 6291456 | tf_op jit(solution)/shard_map/all_to_all | solution.py:157
  336.5 9.0 reduce.38
  354.4 30.8 %all-reduce.10 = (bf16[1024]{0:T(1024)(128)(2,1)S(1)}, bf16[1024]{0:T(1024)(128)(2,1)S(1)}) all-reduce(bf16[1024]{0:T(1024)(128)(2,1)S(1)} %dynamic-update-slice, bf16[1024]{0:T(1024)(128)(2,1)S(1)} %dynamic-update-slice.1), channel_id=1, replica_groups=mesh['fsdp'=16,'seq'=2] {'fsdp'}, use_global_device_ids=true, to_apply=%add | all-reduce | flops 2048 | bytes 8192
  385.2 17.2 %all-gather.2 = bf16[16,1,256]{2,1,0:T(2,128)(2,1)S(1)} all-gather(bf16[1,1,256]{2,1,0:T(2,128)(2,1)S(1)} %reshape.510), channel_id=1, replica_groups=mesh['fsdp'=16,'seq'=2] {'fsdp'}, dimensions={0}, use_global_device_ids=true | all-gather | bytes 8704 | tf_op jit(solution)/shard_map/all_gather | solution.py:136
  416.9 12.0 fusion.122
  428.9 14.3 convert_reduce_fusion
  449.4 12.6 convert_reduce_fusion.3
  476.9 9.3 all-to-all-done.2
  521.1 37.1 %fusion.64 = bf16[8,64,512]{2,1,0:T(8,128)(2,1)} fusion(bf16[1024,8,64]{0,2,1:T(8,128)(2,1)S(1)} %bitcast.199, f32[8,512,1024]{2,1,0:T(8,128)} %fusion.90, f32[8,512]{1,0:T(8,128)S(1)} %log_add_fusion, f32[8,512,1024]{2,1,0:T(8,128)} %copy-done), kind=kOutput, calls=%fused_computation.90 | convolution fusion | flops 574886912 | bytes 35143680 | tf_op jit(solution)/shard_map/bhqk,bkhd->bqhd/dot_general | solution.py:74
  569.8 36.6 %fusion.67 = bf16[8,64,512]{2,1,0:T(8,128)(2,1)S(1)} fusion(bf16[1024,8,64]{0,2,1:T(8,128)(2,1)S(1)} %bitcast.200, f32[8,512,1024]{2,1,0:T(8,128)} %fusion.89, f32[8,512]{1,0:T(8,128)S(1)} %log_add_fusion.1, f32[8,512,1024]{2,1,0:T(8,128)} %get-tuple-element.67), kind=kOutput, calls=%fused_computation.91 | convolution fusion | flops 574886912 | bytes 35143680 | tf_op jit(solution)/shard_map/bhqk,bkhd->bqhd/dot_general | solution.py:74
  608.5 30.7 %fusion.11 = f32[8,64,1024]{2,1,0:T(8,128)} fusion(f32[8,512,1024]{2,1,0:T(8,128)} %fusion.89, f32[8,512,1024]{2,1,0:T(8,128)} %get-tuple-element.67, f32[8,512]{1,0:T(8,128)S(1)} %log_add_fusion.1, bf16[1,1024,8,64]{1,3,2,0:T(8,128)(2,1)S(1)} %bitcast.210), kind=kOutput, calls=%fused_computation.21 | convolution fusion | flops 574624768 | bytes 69763072 | tf_op jit(solution)/shard_map/bhqk,bqhd->bkhd/dot_general | solution.py:76
  639.2 31.5 %add_convert_fusion.2 = bf16[8,64,1024]{2,1,0:T(8,128)(2,1)} fusion(f32[8,64,1024]{2,1,0:T(8,128)} %fusion.11, f32[8,512,1024]{2,1,0:T(8,128)} %fusion.90, f32[8,512]{1,0:T(8,128)S(1)} %log_add_fusion, f32[8,512,1024]{2,1,0:T(8,128)} %copy-done, bf16[1,1024,8,64]{1,3,2,0:T(8,128)(2,1)} %bitcast.208), kind=kOutput, calls=%fused_computation.82 | convolution fusion | flops 575673344 | bytes 70811648 | tf_op jit(solution)/shard_map/bhqk,bqhd->bkhd/dot_general | solution.py:76
  685.2 50.4 %all_to_all.64 = bf16[1,1024,3,1,512]{4,2,3,0,1:T(4,128)(2,1)S(1)} all-to-all(bf16[1,1024,3,1,512]{4,2,3,0,1:T(4,128)(2,1)S(1)} %pad_maximum_fusion), channel_id=1, replica_groups=mesh['fsdp'=16,'seq'=2] {'seq'}, dimensions={1} | all-to-all | bytes 6291456 | tf_op jit(solution)/shard_map/all_to_all | solution.py:222
  739.3 10.5 fusion.117
  749.9 18.8 %fusion.79 = f32[4096,1024]{1,0:T(8,128)} fusion(bf16[1,512,1024]{2,1,0:T(8,128)(2,1)} %param.25, f32[1024]{0:T(1024)S(1)} %bitcast.243, f32[512,4096]{1,0:T(8,128)} %fusion.122, f32[4096]{0:T(1024)S(1)} %bitcast.236), kind=kOutput, calls=%fused_computation.102 | convolution fusion | flops 4317511680 | bytes 26234880 | tf_op jit(solution)/shard_map/btf,btd->fd/dot_general | solution.py:193
  769.4 14.9 %fusion.120 = f32[1024,4096]{1,0:T(8,128)} fusion(bf16[512,4096]{1,0:T(8,128)(2,1)} %copy-done.39, f32[1,512,1024]{2,1,0:T(8,128)} %copy-done.9, f32[1024]{0:T(1024)S(1)} %bitcast.240, f32[1024]{0:T(1024)S(1)} %bitcast.230, f32[512]{0:T(512)S(1)} %add_rsqrt_fusion, f32[512]{0:T(512)S(1)} %broadcast_multiply_fusion.4), kind=kOutput, calls=%fused_computation.181 | convolution fusion | flops 4297588736 | bytes 23080960 | tf_op jit(solution)/shard_map/btd,btf->df/dot_general | solution.py:197
  786.7 61.4 %all-reduce.7 = (f32[2048]{0:T(1024)S(1)}, f32[1024]{0:T(1024)S(1)}, f32[4096]{0:T(1024)S(1)}, f32[1024]{0:T(1024)S(1)}) all-reduce(f32[2048]{0:T(1024)S(1)} %pad_maximum_fusion.2, f32[1024]{0:T(1024)S(1)} %get-tuple-element.47, f32[4096]{0:T(1024)S(1)} %copy-done.23, ...), channel_id=5, replica_groups=mesh['fsdp'=16,'seq'=2] {'fsdp'}, use_global_device_ids=true, to_apply=%region_26.27.clone | all-reduce | flops 8192 | bytes 65536
  859.2 9.5 all-reduce.8
  884.7 180.7 %reduce-scatter.14.cloned.1.call-done = f32[256,1024]{1,0:T(8,128)} async-done(((f32[4096,1024]{1,0:T(8,128)}), f32[256,1024]{1,0:T(8,128)}) %reduce-scatter.14.cloned.1.call-update) | async-done | bytes 1048592 | tf_op jit(solution)/shard_map/reduce_scatter | solution.py:255
  1065.4 180.6 %reduce-scatter.12.cloned.1.call-done = f32[64,4096]{1,0:T(8,128)} async-done(((f32[1024,4096]{1,0:T(8,128)}), f32[64,4096]{1,0:T(8,128)}) %reduce-scatter.12.cloned.1.call-update) | async-done | bytes 1048592 | tf_op jit(solution)/shard_map/reduce_scatter | solution.py:253
  1246.6 61.3 %all-reduce.2 = bf16[6144]{0:T(1024)(128)(2,1)S(1)} all-reduce(bf16[6144]{0:T(1024)(128)(2,1)S(1)} %convert_reduce_fusion.5), channel_id=3, replica_groups=mesh['fsdp'=16,'seq'=2] {'fsdp'}, use_global_device_ids=true, to_apply=%region_22.23.clone | all-reduce | flops 6144 | bytes 24576
  1317.2 67.1 %reduce-scatter.6.cloned.1.call-done = bf16[64,6144]{1,0:T(8,128)(2,1)} async-done(((bf16[1024,6144]{1,0:T(8,128)(2,1)}), bf16[64,6144]{1,0:T(8,128)(2,1)}) %reduce-scatter.6.cloned.1.call-update) | async-done | bytes 786448 | tf_op jit(solution)/shard_map/reduce_scatter | solution.py:241
  1386.7 85.1 %all-reduce.13.cloned.1.call-done = (f32[64,3072]{1,0:T(8,128)}, f32[64,1024]{1,0:T(8,128)}, f32[64,4096]{1,0:T(8,128)}, f32[256,1024]{1,0:T(8,128)}) async-done(((f32[64,3072]{1,0:T(8,128)}, f32[64,1024]{1,0:T(8,128)}, f32[64,4096]{1,0:T(8,128)}, f32[256,1024]{1,0:T(8,128)}), (f32[64,3072]{1,0:T(8,128)}, f32[64,1024]{1,0:T(8,128)}, f32[64,4096]{1,0:T(8,128)}, ...) | async-done | bytes 3145744 | tf_op jit(solution)/shard_map/psum | solution.py:259
  (251 shorter events, 293.8 us)
Async XLA Ops:
  7.2 229.4 %all-gather.8.cloned.1.call-start = ((), (), s32[]{:S(2)}) async-start(), calls=%async_computation.9 | async-start | bytes 6684672 | tf_op jit(solution)/shard_map/all_gather | solution.py:131
  7.9 402.7 %all-gather.10.cloned.1.call-start = ((), (), s32[]{:S(2)}) async-start(), calls=%async_computation.10 | async-start | bytes 2228224 | tf_op jit(solution)/shard_map/all_gather | solution.py:133
  8.7 408.2 %all-gather.12.cloned.1.call-start = ((), (), s32[]{:S(2)}) async-start(), calls=%async_computation.11 | async-start | bytes 8912896 | tf_op jit(solution)/shard_map/all_gather | solution.py:135
  9.4 419.5 %all-gather.14.cloned.1.call-start = ((), (), s32[]{:S(2)}) async-start(), calls=%async_computation.12 | async-start | bytes 8912896 | tf_op jit(solution)/shard_map/all_gather | solution.py:137
  9.5 64.5 %collective-permute-start.1 = (bf16[64,6144]{1,0:T(8,128)(2,1)}, bf16[64,6144]{1,0:T(8,128)(2,1)S(1)}, u32[]{:S(2)}, u32[]{:S(2)}) collective-permute-start(bf16[64,6144]{1,0:T(8,128)(2,1)} %param.15), channel_id=1, source_target_pairs={{0,30},{2,0},{4,2},{6,4},{8,6},{10,8},{12,10},{14,12},{16,14},{18,... | collective-permute-start | bytes 2359304 | tf_op jit(solution)/shard_map/ppermute | solution.py:122
  15.0 59.8 %collective-permute-start = (bf16[64,6144]{1,0:T(8,128)(2,1)}, bf16[64,6144]{1,0:T(8,128)(2,1)S(1)}, u32[]{:S(2)}, u32[]{:S(2)}) collective-permute-start(bf16[64,6144]{1,0:T(8,128)(2,1)} %param.15), channel_id=1, source_target_pairs={{0,2},{2,4},{4,6},{6,8},{8,10},{10,12},{12,14},{14,16},{16,18},{18... | collective-permute-start | bytes 2359304 | tf_op jit(solution)/shard_map/ppermute | solution.py:117
  17.4 219.2 %copy-start.18 = (f32[512]{0:T(512)}, f32[512]{0:T(512)S(1)}, u32[]{:S(2)}) copy-start(f32[512]{0:T(512)S(1)} %broadcast_multiply_fusion.5) | copy-start | bytes 6148
  19.1 217.5 %copy-start.24 = (f32[512]{0:T(512)}, f32[512]{0:T(512)S(1)}, u32[]{:S(2)}) copy-start(f32[512]{0:T(512)S(1)} %add_rsqrt_fusion.1) | copy-start | bytes 6148
  74.0 10.3 collective-permute-start.3
  74.8 14.2 collective-permute-start.2
  84.3 20.9 %collective-permute-start.5 = (bf16[64,6144]{1,0:T(8,128)(2,1)S(1)}, bf16[64,6144]{1,0:T(8,128)(2,1)S(1)}, u32[]{:S(2)}, u32[]{:S(2)}) collective-permute-start(bf16[64,6144]{1,0:T(8,128)(2,1)S(1)} %collective-permute-done.3), channel_id=1, source_target_pairs={{0,30},{2,0},{4,2},{6,4},{8,6},{10,8},{12,10},{14,12},{16,14},{18,... | collective-permute-start | bytes 2359304 | tf_op jit(solution)/shard_map/ppermute | solution.py:122
  89.0 18.1 %collective-permute-start.4 = (bf16[64,6144]{1,0:T(8,128)(2,1)S(1)}, bf16[64,6144]{1,0:T(8,128)(2,1)S(1)}, u32[]{:S(2)}, u32[]{:S(2)}) collective-permute-start(bf16[64,6144]{1,0:T(8,128)(2,1)S(1)} %collective-permute-done.2), channel_id=1, source_target_pairs={{0,2},{2,4},{4,6},{6,8},{8,10},{10,12},{12,14},{14,16},{16,18},{18... | collective-permute-start | bytes 2359304 | tf_op jit(solution)/shard_map/ppermute | solution.py:117
  105.2 124.8 %copy-start.14 = (bf16[1,1024]{1,0:T(2,128)(2,1)S(1)}, bf16[1,1024]{1,0:T(2,128)(2,1)}, u32[]{:S(2)}) copy-start(bf16[1,1024]{1,0:T(2,128)(2,1)} %param.14) | copy-start | bytes 6148
  105.2 24.0 %collective-permute-start.7 = (bf16[64,6144]{1,0:T(8,128)(2,1)S(1)}, bf16[64,6144]{1,0:T(8,128)(2,1)S(1)}, u32[]{:S(2)}, u32[]{:S(2)}) collective-permute-start(bf16[64,6144]{1,0:T(8,128)(2,1)S(1)} %collective-permute-done.5), channel_id=1, source_target_pairs={{0,30},{2,0},{4,2},{6,4},{8,6},{10,8},{12,10},{14,12},{16,14},{18,... | collective-permute-start | bytes 2359304 | tf_op jit(solution)/shard_map/ppermute | solution.py:122
  107.1 22.1 %collective-permute-start.6 = (bf16[64,6144]{1,0:T(8,128)(2,1)S(1)}, bf16[64,6144]{1,0:T(8,128)(2,1)S(1)}, u32[]{:S(2)}, u32[]{:S(2)}) collective-permute-start(bf16[64,6144]{1,0:T(8,128)(2,1)S(1)} %collective-permute-done.4), channel_id=1, source_target_pairs={{0,2},{2,4},{4,6},{6,8},{8,10},{10,12},{12,14},{14,16},{16,18},{18... | collective-permute-start | bytes 2359304 | tf_op jit(solution)/shard_map/ppermute | solution.py:117
  129.2 19.4 %collective-permute-start.9 = (bf16[64,6144]{1,0:T(8,128)(2,1)S(1)}, bf16[64,6144]{1,0:T(8,128)(2,1)S(1)}, u32[]{:S(2)}, u32[]{:S(2)}) collective-permute-start(bf16[64,6144]{1,0:T(8,128)(2,1)S(1)} %collective-permute-done.7), channel_id=1, source_target_pairs={{0,30},{2,0},{4,2},{6,4},{8,6},{10,8},{12,10},{14,12},{16,14},{18,... | collective-permute-start | bytes 2359304 | tf_op jit(solution)/shard_map/ppermute | solution.py:122
  129.2 19.5 %collective-permute-start.8 = (bf16[64,6144]{1,0:T(8,128)(2,1)S(1)}, bf16[64,6144]{1,0:T(8,128)(2,1)S(1)}, u32[]{:S(2)}, u32[]{:S(2)}) collective-permute-start(bf16[64,6144]{1,0:T(8,128)(2,1)S(1)} %collective-permute-done.6), channel_id=1, source_target_pairs={{0,2},{2,4},{4,6},{6,8},{8,10},{10,12},{12,14},{14,16},{16,18},{18... | collective-permute-start | bytes 2359304 | tf_op jit(solution)/shard_map/ppermute | solution.py:117
  148.6 23.9 %collective-permute-start.11 = (bf16[64,6144]{1,0:T(8,128)(2,1)S(1)}, bf16[64,6144]{1,0:T(8,128)(2,1)S(1)}, u32[]{:S(2)}, u32[]{:S(2)}) collective-permute-start(bf16[64,6144]{1,0:T(8,128)(2,1)S(1)} %collective-permute-done.9), channel_id=1, source_target_pairs={{0,30},{2,0},{4,2},{6,4},{8,6},{10,8},{12,10},{14,12},{16,14},{18,... | collective-permute-start | bytes 2359304 | tf_op jit(solution)/shard_map/ppermute | solution.py:122
  148.7 29.9 %collective-permute-start.10 = (bf16[64,6144]{1,0:T(8,128)(2,1)S(1)}, bf16[64,6144]{1,0:T(8,128)(2,1)S(1)}, u32[]{:S(2)}, u32[]{:S(2)}) collective-permute-start(bf16[64,6144]{1,0:T(8,128)(2,1)S(1)} %collective-permute-done.8), channel_id=1, source_target_pairs={{0,2},{2,4},{4,6},{6,8},{8,10},{10,12},{12,14},{14,16},{16,18},{18... | collective-permute-start | bytes 2359304 | tf_op jit(solution)/shard_map/ppermute | solution.py:117
  172.5 48.1 %collective-permute-start.13 = (bf16[64,6144]{1,0:T(8,128)(2,1)S(1)}, bf16[64,6144]{1,0:T(8,128)(2,1)S(1)}, u32[]{:S(2)}, u32[]{:S(2)}) collective-permute-start(bf16[64,6144]{1,0:T(8,128)(2,1)S(1)} %collective-permute-done.11), channel_id=1, source_target_pairs={{0,30},{2,0},{4,2},{6,4},{8,6},{10,8},{12,10},{14,12},{16,14},{18,... | collective-permute-start | bytes 2359304 | tf_op jit(solution)/shard_map/ppermute | solution.py:122
  178.6 30.8 %collective-permute-start.12 = (bf16[64,6144]{1,0:T(8,128)(2,1)S(1)}, bf16[64,6144]{1,0:T(8,128)(2,1)S(1)}, u32[]{:S(2)}, u32[]{:S(2)}) collective-permute-start(bf16[64,6144]{1,0:T(8,128)(2,1)S(1)} %collective-permute-done.10), channel_id=1, source_target_pairs={{0,2},{2,4},{4,6},{6,8},{8,10},{10,12},{12,14},{14,16},{16,18},{18... | collective-permute-start | bytes 2359304 | tf_op jit(solution)/shard_map/ppermute | solution.py:117
  209.4 19.7 %collective-permute-start.14 = (bf16[64,6144]{1,0:T(8,128)(2,1)S(1)}, bf16[64,6144]{1,0:T(8,128)(2,1)S(1)}, u32[]{:S(2)}, u32[]{:S(2)}) collective-permute-start(bf16[64,6144]{1,0:T(8,128)(2,1)S(1)} %collective-permute-done.12), channel_id=1, source_target_pairs={{0,2},{2,4},{4,6},{6,8},{8,10},{10,12},{12,14},{14,16},{16,18},{18... | collective-permute-start | bytes 2359304 | tf_op jit(solution)/shard_map/ppermute | solution.py:117
  236.6 180.4 %copy-start.26 = (f32[1,1,1024]{2,1,0:T(1,128)}, f32[1,1,1024]{2,1,0:T(1,128)S(1)}, u32[]{:S(2)}) copy-start(f32[1,1,1024]{2,1,0:T(1,128)S(1)} %get-tuple-element.53) | copy-start | bytes 12292
  335.9 74.7 %copy-start.3 = (bf16[1,512,1024]{2,1,0:T(8,128)(2,1)S(1)}, bf16[1,512,1024]{2,1,0:T(8,128)(2,1)}, u32[]{:S(2)}) copy-start(bf16[1,512,1024]{2,1,0:T(8,128)(2,1)} %param.13) | copy-start | bytes 3145732
  348.1 54.3 %all-to-all-start.1 = ((bf16[2,2,131072]{2,1,0:T(2,128)(2,1)}), bf16[2,2,131072]{2,1,0:T(2,128)(2,1)}, u32[]{:S(2)}, u32[]{:S(2)}) async-start(bf16[2,2,131072]{2,1,0:T(2,128)(2,1)} %reshape.533), calls=%async_computation.1 | async-start | bytes 2097152 | tf_op jit(solution)/shard_map/all_to_all | solution.py:169
  468.2 18.0 %all-to-all-start.2 = ((bf16[1,512,2,512]{3,1,0,2:T(8,128)(2,1)}), bf16[1,512,2,512]{3,1,0,2:T(8,128)(2,1)S(1)}, u32[]{:S(2)}, u32[]{:S(2)}) async-start(bf16[1,512,2,512]{3,1,0,2:T(8,128)(2,1)} %copy.53), calls=%async_computation.2 | async-start | bytes 2097152 | tf_op jit(solution)/shard_map/all_to_all | solution.py:210
  471.8 404.5 %reduce-scatter.10.cloned.1.call-start = ((), (), s32[]{:S(2)}) async-start(), calls=%async_computation.15 | async-start | bytes 4456448 | tf_op jit(solution)/shard_map/reduce_scatter | solution.py:251
  476.8 407.9 %reduce-scatter.8.cloned.1.call-start = ((), (), s32[]{:S(2)}) async-start(), calls=%async_computation.14 | async-start | bytes 13369344 | tf_op jit(solution)/shard_map/reduce_scatter | solution.py:249
  749.8 315.6 %reduce-scatter.14.cloned.1.call-start = ((), (), s32[]{:S(2)}) async-start(), calls=%async_computation.17 | async-start | bytes 17825792 | tf_op jit(solution)/shard_map/reduce_scatter | solution.py:255
  768.7 477.3 %reduce-scatter.12.cloned.1.call-start = ((), (), s32[]{:S(2)}) async-start(), calls=%async_computation.16 | async-start | bytes 17825792 | tf_op jit(solution)/shard_map/reduce_scatter | solution.py:253
  784.3 600.0 %reduce-scatter.6.cloned.1.call-start = ((), (), s32[]{:S(2)}) async-start(), calls=%async_computation.13 | async-start | bytes 13369344 | tf_op jit(solution)/shard_map/reduce_scatter | solution.py:241
  876.2 595.5 %all-reduce.13.cloned.1.call-start = ((), (), s32[]{:S(2)}) async-start(), calls=%async_computation.18 | async-start | bytes 6291456 | tf_op jit(solution)/shard_map/psum | solution.py:259
  (35 other events, 465.8 us)
Sparse Core Ops, SparseCore 0:
  10.3 69.8 all-gather.7
  82.3 55.6 all-gather.9
  140.1 103.9 all-gather.11
  246.2 73.1 all-gather.13
  476.9 72.0 reduce-scatter.9
  749.9 134.6 reduce-scatter.7
  888.8 176.5 reduce-scatter.13
  1069.5 176.4 reduce-scatter.11
  1250.0 134.2 reduce-scatter.5
  1386.6 85.1 all-reduce.12
